TPU v7x, 128 devices: a whole 4x4x4 slice. The times are simulated.
128 devices in a mesh: freq: 8 (over z, x_hi), rcv: 16 (over x_lo, y, core).
Axes of the slice: x: 4 (x_hi: 2, x_lo: 2; x = x_hi * 2 + x_lo), y: 4, z: 4, core: 2. Of those that a mesh axis runs over, the one named last changes fastest.
Arguments:
- reflection: float32 [128, 2, 1024, 2048], P('freq', None, None, 'rcv'), may hold values from -0.09375 to 0.09375
- focusing_input: float32 [128, 2, 32, 2048], P('freq', None, None, 'rcv'), may hold values from -6 to 6
- direct_wave: float32 [256, 32, 2048], P(None, 'freq', 'rcv'), may hold values from -6 to 6
- mute_source: int32 [32, 1024], P('rcv', 'freq'), may hold values from 32 to 127
- mute_receiver: int32 [32, 2048], P('freq', 'rcv'), may hold values from 32 to 127
Outputs:
- focus_minus: float32 [256, 32, 1024], P(None, 'rcv', 'freq')
- focus_plus: float32 [256, 32, 2048], P(None, 'freq', 'rcv')
All inputs are finite; a program needn't handle non-finite values.
Results may differ from a plain program's by a relative error of at most 0.00007.
Values sent between devices are 32-bit elements; how exact they have to be, the bound alone decides.
No kernel may reach another device: no remote copies, remote signals or barrier semaphores. Data moves between devices by JAX's collectives and lax.ppermute only.
A program may use at most 128 MiB of HBM per device.

v0:
```python
import math
import jax
import jax.numpy as jnp
from jax import lax
from jax.sharding import PartitionSpec as P

MAXIMUM_ACCURACY = lax.Precision.HIGHEST


def dft_tables(freqs, samples):
    index_freq = lax.broadcasted_iota(jnp.int32, (freqs, samples), 0) + 1
    index_time = lax.broadcasted_iota(jnp.int32, (freqs, samples), 1)
    phase_turns = jnp.mod(index_freq * index_time, samples).astype(jnp.float32) * (
        2.0 * math.pi / samples
    )
    return (jnp.cos(phase_turns), jnp.sin(phase_turns))


def window(traces, mute_table):
    samples = traces.shape[0]
    time_index = lax.broadcasted_iota(jnp.int32, (samples, 1, 1), 0)
    kept_mask = (time_index < mute_table[None]) | (time_index > samples - mute_table[None])
    return jnp.where(kept_mask, traces, jnp.zeros_like(traces))


def forward_panel(reflection, focusing_input):
    reflection_real = reflection[:, 0]
    reflection_imaginary = reflection[:, 1]
    real_part = jnp.einsum(
        "ual,uel->eua", reflection_real, focusing_input[:, 0], precision=MAXIMUM_ACCURACY
    ) - jnp.einsum(
        "ual,uel->eua", reflection_imaginary, focusing_input[:, 1], precision=MAXIMUM_ACCURACY
    )
    imag_part = jnp.einsum(
        "ual,uel->eua", reflection_real, focusing_input[:, 1], precision=MAXIMUM_ACCURACY
    ) + jnp.einsum(
        "ual,uel->eua", reflection_imaginary, focusing_input[:, 0], precision=MAXIMUM_ACCURACY
    )
    return jnp.stack((real_part, imag_part), axis=2)


def adjoint_panel(reflection, receiver_panel):
    reflection_real = reflection[:, 0]
    reflection_imaginary = reflection[:, 1]
    real_part = jnp.einsum(
        "klh,lhc->klc", receiver_panel[:, :, 0], reflection_real, precision=MAXIMUM_ACCURACY
    ) + jnp.einsum(
        "klh,lhc->klc", receiver_panel[:, :, 1], reflection_imaginary, precision=MAXIMUM_ACCURACY
    )
    imag_part = jnp.einsum(
        "klh,lhc->klc", receiver_panel[:, :, 1], reflection_real, precision=MAXIMUM_ACCURACY
    ) - jnp.einsum(
        "klh,lhc->klc", receiver_panel[:, :, 0], reflection_imaginary, precision=MAXIMUM_ACCURACY
    )
    return jnp.stack((real_part, imag_part), axis=2)


def to_time(spectrum, cosine, sine_table, factor):
    return factor * (
        jnp.einsum("akb,kt->tab", spectrum[:, :, 0], cosine, precision=MAXIMUM_ACCURACY)
        - jnp.einsum("akb,kt->tab", spectrum[:, :, 1], sine_table, precision=MAXIMUM_ACCURACY)
    )


def to_freq(traces, cosine, sine_table, factor):
    real_part = factor * jnp.einsum("tab,kt->akb", traces, cosine, precision=MAXIMUM_ACCURACY)
    imag_part = -factor * jnp.einsum("tab,kt->akb", traces, sine_table, precision=MAXIMUM_ACCURACY)
    return jnp.stack((real_part, imag_part), axis=2)


def body(reflection, focusing_input, direct_wave, mute_source, mute_receiver):
    freqs = reflection.shape[0] * lax.axis_size("freq")
    samples = 2 * freqs
    factor = 1.0 / math.sqrt(freqs)
    cosine, sine_table = dft_tables(freqs, samples)
    share = mute_source.shape[0]
    term = forward_panel(reflection, focusing_input)
    summed = lax.psum(term, "rcv")
    spectrum = lax.all_to_all(summed, "freq", split_axis=3, concat_axis=1, tiled=True)
    mutes_all = lax.all_gather(mute_source, "rcv", axis=0, tiled=True)
    windowed = window(to_time(spectrum, cosine, sine_table, factor), mutes_all)
    focus_minus = lax.dynamic_slice_in_dim(windowed, lax.axis_index("rcv") * share, share, 1)
    back_local = to_freq(windowed, cosine, sine_table, factor)
    back_spec = lax.all_to_all(back_local, "freq", split_axis=1, concat_axis=3, tiled=True)
    adjoint = adjoint_panel(reflection, back_spec)
    receiver_spec = lax.all_to_all(adjoint, "freq", split_axis=0, concat_axis=1, tiled=True)
    adj_time = to_time(receiver_spec, cosine, sine_table, factor)
    focus_plus = direct_wave - window(adj_time, mute_receiver)
    return (focus_minus, focus_plus)


def solution(mesh):
    placed = (
        P("freq", None, None, "rcv"),
        P("freq", None, None, "rcv"),
        P(None, "freq", "rcv"),
        P("rcv", "freq"),
        P("freq", "rcv"),
    )
    return jax.shard_map(
        body,
        mesh=mesh,
        in_specs=placed,
        out_specs=(P(None, "rcv", "freq"), P(None, "freq", "rcv")),
        check_vma=False,
    )
```

profile of v0, /device:TPU:0, one launch (start us, length us, event | category | flops | bytes accessed | tf_op | source)
XLA Modules:
  0.0 455.7 jit_solution(1087763690156176081)
XLA Ops:
  7.2 0.0 all-reduce.2.cloned.1.call-start
  7.2 0.0 copy-start
  7.2 10.8 %fusion.4 = f32[16,32,1024]{2,1,0:T(8,128)S(1)} fusion(f32[16,2,1024,128]{3,2,1,0:T(8,128)} %param.5, f32[16,2,32,128]{3,2,1,0:T(8,128)} %param.6), kind=kOutput, calls=%fused_computation.4 | convolution fusion | flops 805306368 | bytes 10747904 | tf_op jit(solution)/shard_map/ual,uel->eua/dot_general | solution.py:36
  18.1 11.1 %fusion.6 = f32[16,32,1024]{2,1,0:T(8,128)S(1)} fusion(f32[16,2,1024,128]{3,2,1,0:T(8,128)} %param.5, f32[16,2,32,128]{3,2,1,0:T(8,128)S(1)} %copy-done.4), kind=kOutput, calls=%fused_computation.6 | convolution fusion | flops 805306368 | bytes 10747904 | tf_op jit(solution)/shard_map/ual,uel->eua/dot_general | solution.py:31
  29.2 0.0 copy-done
  29.2 8.4 %add_bitcast_fusion = f32[32,16,1,1024]{3,0,1,2:T(8,128)S(1)} fusion(f32[16,32,1024]{2,1,0:T(8,128)S(1)} %fusion.4, f32[16,2,1024,128]{3,2,1,0:T(8,128)S(1)} %copy-done, f32[16,2,32,128]{3,2,1,0:T(8,128)S(1)} %copy-done.4), kind=kOutput, calls=%fused_computation.38 | convolution fusion | flops 805830656 | bytes 12845056 | tf_op jit(solution)/shard_map/ual,uel->eua/dot_general | solution.py:34
  37.6 8.6 %subtract_bitcast_fusion = f32[32,16,1,1024]{3,0,1,2:T(8,128)S(1)} fusion(f32[16,32,1024]{2,1,0:T(8,128)S(1)} %fusion.6, f32[16,2,1024,128]{3,2,1,0:T(8,128)S(1)} %copy-done, f32[16,2,32,128]{3,2,1,0:T(8,128)S(1)} %copy-done.4), kind=kOutput, calls=%fused_computation.39 | convolution fusion | flops 805830656 | bytes 12845056 | tf_op jit(solution)/shard_map/ual,uel->eua/dot_general | solution.py:29
  46.2 2.6 pad_maximum_fusion
  48.8 0.0 all-reduce.2.cloned.1.call-update
  48.8 132.0 %all-reduce.2.cloned.1.call-done = f32[32,16,2,1024]{3,0,1,2:T(8,128)} async-done(((f32[32,16,2,1024]{3,0,1,2:T(8,128)}), f32[32,16,2,1024]{3,0,1,2:T(8,128)}) %all-reduce.2.cloned.1.call-update) | async-done | bytes 4194320 | tf_op jit(solution)/shard_map/psum | solution.py:78
  180.8 14.3 %copy.23 = f32[32,16,2,1024]{0,1,2,3:T(8,128)} copy(f32[32,16,2,1024]{3,0,1,2:T(8,128)} %all-reduce.2.cloned.1.call-done) | data formatting | bytes 8388608 | tf_op jit(solution)/shard_map/psum | solution.py:78
  195.1 12.8 %reshape.16 = f32[8,1,131072]{2,1,0:T(1,128)} reshape(f32[1024,2,16,32]{3,2,1,0:T(8,128)} %bitcast.140) | data formatting | bytes 8388608
  207.9 6.7 %all-to-all-start = ((f32[8,1,131072]{2,1,0:T(1,128)}), f32[8,1,131072]{2,1,0:T(1,128)}, u32[]{:S(2)}, u32[]{:S(2)}) async-start(f32[8,1,131072]{2,1,0:T(1,128)} %reshape.16), calls=%async_computation | async-start | bytes 8388608 | tf_op jit(solution)/shard_map/all_to_all | solution.py:79
  214.6 0.0 copy-done.7
  214.6 58.8 %all-gather = s32[16,2,128]{2,1,0:T(2,128)S(1)} all-gather(s32[1,2,128]{2,1,0:T(2,128)S(1)} %bitcast.151), channel_id=1, replica_groups=mesh['freq'=8,'rcv'=16] {'rcv'}, dimensions={0}, use_global_device_ids=true | all-gather | bytes 17408 | tf_op jit(solution)/shard_map/all_gather | solution.py:80
  273.4 0.0 all-to-all-done
  273.5 0.5 broadcast.42
  274.0 13.7 %reduce = f32[8,131072]{1,0:T(8,128)} reduce(f32[8,1,131072]{2,1,0:T(1,128)} %all-to-all-done, f32[]{:T(128)} %broadcast.42), dimensions={1}, to_apply=%all_to_all.39.reduce_sub_computation | reduce | bytes 8388612 | tf_op jit(solution)/shard_map/all_to_all | solution.py:79
  287.7 13.4 %reshape.17 = f32[1024,2,16,32]{3,2,1,0:T(8,128)} reshape(f32[8,131072]{1,0:T(8,128)} %reduce) | data formatting | bytes 8388608
  301.0 13.5 %copy.24 = f32[32,16,2,8,128]{4,1,3,0,2:T(8,128)} copy(f32[32,16,2,8,128]{0,1,2,4,3:T(8,128)} %bitcast.141) | data formatting | bytes 8388608 | tf_op jit(solution)/shard_map/all_to_all | solution.py:79
  314.6 0.0 copy-start.3
  314.6 5.8 %fusion.25 = f32[256,32,128]{2,0,1:T(8,128)S(1)} fusion(f32[32,128,2,128]{3,1,0,2:T(8,128)} %bitcast.142, s32[128]{0:T(128)S(1)} %iota_add_fusion), kind=kOutput, calls=%fused_computation.35 | convolution fusion | flops 1611071488 | bytes 6291968 | tf_op jit(solution)/shard_map/akb,kt->tab/dot_general | solution.py:60
  320.4 0.0 copy-done.3
  320.4 5.0 %multiply_select_fusion = f32[256,32,128]{2,0,1:T(8,128)S(1)} fusion(f32[256,32,128]{2,0,1:T(8,128)S(1)} %fusion.25, f32[32,128,2,128]{3,1,0,2:T(8,128)S(1)} %bitcast.143, s32[32,128]{1,0:T(8,128)S(1)} %broadcast_subtract_fusion, s32[32,128]{1,0:T(8,128)S(1)} %bitcast.150, s32[128]{0:T(128)S(1)} %iota_add_fusion), kind=kOutput, calls=%fused_computation.27 | convolution fusion | flops 1617362944 | bytes 10519040 | tf_op jit(solution)/shard_map/akb,kt->tab/dot_general | solution.py:61
  325.4 0.0 copy-start.1
  325.4 2.8 multiply_bitcast_fusion
  328.2 3.0 multiply_bitcast_fusion.1
  331.2 0.5 pad_maximum_fusion.1
  331.7 2.4 copy.27
  334.2 58.4 %all_to_all.54 = f32[32,128,2,128]{3,0,2,1:T(8,128)S(1)} all-to-all(f32[32,128,2,128]{3,0,2,1:T(8,128)S(1)} %copy.27), channel_id=1, replica_groups=mesh['freq'=8,'rcv'=16] {'freq'}, dimensions={1} | all-to-all | bytes 8388608 | tf_op jit(solution)/shard_map/all_to_all | solution.py:84
  392.6 5.8 %copy.44 = f32[32,8,16,2,128]{4,1,0,2,3:T(8,128)} copy(f32[32,8,16,2,128]{4,0,3,2,1:T(8,128)S(1)} %bitcast.144) | data formatting | bytes 8388608 | tf_op jit(solution)/shard_map/all_to_all | solution.py:84
  398.4 4.9 %all_to_all.46 = f32[32,16,2,1024]{3,0,1,2:T(8,128)} reshape(f32[32,16,2,8,128]{4,3,0,1,2:T(8,128)} %bitcast.145) | data formatting | bytes 8388608 | tf_op jit(solution)/shard_map/all_to_all | solution.py:84
  403.3 7.3 %fusion = f32[16,32,128]{2,1,0:T(8,128)S(1)} fusion(f32[16,2,1024,128]{3,2,1,0:T(8,128)} %param.5, f32[32,16,2,1024]{3,0,1,2:T(8,128)} %all_to_all.46), kind=kOutput, calls=%fused_computation | convolution fusion | flops 805306368 | bytes 10747904 | tf_op jit(solution)/shard_map/klh,lhc->klc/dot_general | solution.py:52
  410.6 0.0 slice-start.2
  410.6 7.3 %fusion.2 = f32[16,32,128]{2,1,0:T(8,128)S(1)} fusion(f32[16,2,1024,128]{3,2,1,0:T(8,128)} %param.5, f32[32,16,2,1024]{3,0,1,2:T(8,128)} %all_to_all.46), kind=kOutput, calls=%fused_computation.2 | convolution fusion | flops 805306368 | bytes 10747904 | tf_op jit(solution)/shard_map/klh,lhc->klc/dot_general | solution.py:47
  417.9 0.0 slice-start.3
  417.9 7.2 %fusion.42 = f32[32,16,1,128]{3,0,1,2:T(8,128)S(1)} fusion(f32[16,32,128]{2,1,0:T(8,128)S(1)} %fusion, f32[16,2,1024,128]{3,2,1,0:T(8,128)} %param.5, f32[32,16,2,1024]{3,0,1,2:T(8,128)S(1)} %copy-done.2), kind=kOutput, calls=%fused_computation.47 | convolution fusion | flops 805371904 | bytes 11010048 | tf_op jit(solution)/shard_map/klh,lhc->klc/dot_general | solution.py:50
  425.1 0.0 copy-start.6
  425.1 4.5 fusion.36
  429.6 0.0 copy-start.5
  429.6 1.1 copy.29
  430.7 3.5 all-to-all-start.2
  434.3 1.0 constant_dynamic-slice_fusion
  435.2 0.9 copy.32
  436.1 9.0 %all-to-all-done.2 = f32[32,16,2,128]{3,1,2,0:T(8,128)S(1)} async-done(((f32[32,16,2,128]{3,1,2,0:T(8,128)}), f32[32,16,2,128]{3,1,2,0:T(8,128)S(1)}, u32[]{:S(2)}, u32[]{:S(2)}) %all-to-all-start.2) | async-done | bytes 524320 | tf_op jit(solution)/shard_map/all_to_all | solution.py:86
  445.2 1.1 fusion.46
  446.2 1.2 fusion.32
  447.5 1.1 copy.33
  (20 shorter events, 0.1 us)
Async XLA Ops:
  7.2 10.9 %copy-start.4 = (f32[16,2,32,128]{3,2,1,0:T(8,128)S(1)}, f32[16,2,32,128]{3,2,1,0:T(8,128)}, u32[]{:S(2)}) copy-start(f32[16,2,32,128]{3,2,1,0:T(8,128)} %param.6) | copy-start | bytes 1572868
  7.2 173.6 %all-reduce.2.cloned.1.call-start = ((), (), s32[]{:S(2)}) async-start(), calls=%async_computation.3 | async-start | bytes 8388608 | tf_op jit(solution)/shard_map/psum | solution.py:78
  7.2 22.0 %copy-start = (f32[16,2,1024,128]{3,2,1,0:T(8,128)S(1)}, f32[16,2,1024,128]{3,2,1,0:T(8,128)}, u32[]{:S(2)}) copy-start(f32[16,2,1024,128]{3,2,1,0:T(8,128)} %param.5) | copy-start | bytes 50331652
  207.9 6.7 %copy-start.7 = (s32[2,128]{1,0:T(2,128)S(1)}, s32[2,128]{1,0:T(2,128)}, u32[]{:S(2)}) copy-start(s32[2,128]{1,0:T(2,128)} %param.8) | copy-start | bytes 3076
  207.9 65.5 %all-to-all-start = ((f32[8,1,131072]{2,1,0:T(1,128)}), f32[8,1,131072]{2,1,0:T(1,128)}, u32[]{:S(2)}, u32[]{:S(2)}) async-start(f32[8,1,131072]{2,1,0:T(1,128)} %reshape.16), calls=%async_computation | async-start | bytes 8388608 | tf_op jit(solution)/shard_map/all_to_all | solution.py:79
  314.6 5.8 %copy-start.3 = (f32[32,16,2,8,128]{4,1,3,0,2:T(8,128)S(1)}, f32[32,16,2,8,128]{4,1,3,0,2:T(8,128)}, u32[]{:S(2)}) copy-start(f32[32,16,2,8,128]{4,1,3,0,2:T(8,128)} %copy.24) | copy-start | bytes 12582916
  325.4 2.9 copy-start.1
  403.3 21.8 %slice-start = ((s8[16777216]{0:T(1024)(128)(4,1)}), s8[4194304]{0:T(1024)(128)(4,1)S(1)}, s32[]{:S(2)}) async-start(s8[16777216]{0:T(1024)(128)(4,1)} %bitcast.138), calls=%async_computation.4 | async-start | bytes 8388608
  403.3 21.8 %slice-start.1 = ((s8[16777216]{0:T(1024)(128)(4,1)}), s8[4194304]{0:T(1024)(128)(4,1)S(1)}, s32[]{:S(2)}) async-start(s8[16777216]{0:T(1024)(128)(4,1)} %bitcast.138), calls=%async_computation.5 | async-start | bytes 8388608
  410.6 7.3 %copy-start.2 = (f32[32,16,2,1024]{3,0,1,2:T(8,128)S(1)}, f32[32,16,2,1024]{3,0,1,2:T(8,128)}, u32[]{:S(2)}) copy-start(f32[32,16,2,1024]{3,0,1,2:T(8,128)} %all_to_all.46) | copy-start | bytes 12582916
  410.6 14.5 %slice-start.2 = ((s8[16777216]{0:T(1024)(128)(4,1)}), s8[4194304]{0:T(1024)(128)(4,1)S(1)}, s32[]{:S(2)}) async-start(s8[16777216]{0:T(1024)(128)(4,1)} %bitcast.138), calls=%async_computation.6 | async-start | bytes 8388608
  417.9 7.2 %slice-start.3 = ((s8[16777216]{0:T(1024)(128)(4,1)}), s8[4194304]{0:T(1024)(128)(4,1)S(1)}, s32[]{:S(2)}) async-start(s8[16777216]{0:T(1024)(128)(4,1)} %bitcast.138), calls=%async_computation.7 | async-start | bytes 8388608
  425.1 9.2 %copy-start.6 = (s32[4,128]{1,0:T(4,128)S(1)}, s32[4,128]{1,0:T(4,128)}, u32[]{:S(2)}) copy-start(s32[4,128]{1,0:T(4,128)} %param.9) | copy-start | bytes 6148
  429.6 16.6 %copy-start.5 = (f32[256,4,128]{2,1,0:T(4,128)S(1)}, f32[256,4,128]{2,1,0:T(4,128)}, u32[]{:S(2)}) copy-start(f32[256,4,128]{2,1,0:T(4,128)} %param.7) | copy-start | bytes 1572868
  430.7 14.4 %all-to-all-start.2 = ((f32[32,16,2,128]{3,1,2,0:T(8,128)}), f32[32,16,2,128]{3,1,2,0:T(8,128)S(1)}, u32[]{:S(2)}, u32[]{:S(2)}) async-start(f32[32,16,2,128]{3,1,2,0:T(8,128)} %copy.29), calls=%async_computation.2 | async-start | bytes 1048576 | tf_op jit(solution)/shard_map/all_to_all | solution.py:86
Sparse Core Ops, SparseCore 0:
  48.9 131.7 all-reduce.1
where the time goes:
time: 462 us; the launch traced here: 456 us
  waiting for transfers between devices  141 us (31%)
  blocking collectives  117 us (25%)
  matrix products  84 us (18%)
  local copies, waits for them, and re-layouts  71.9 us (16%)
  other arithmetic  16.8 us (4%)
  between operations  14.6 us (3%)
  starting transfers between devices  10.2 us (2%)
    psum x1, waiting for transfers between devices, body(): summed = lax.psum(term, 'rcv')  132 us
    all_gather x1, blocking collectives, body(): mutes_all = lax.all_gather(mute_source, 'rcv', axis=0, tiled=True)  58.8 us
    all_to_all x1, blocking collectives, body(): lax.all_to_all(back_local, 'freq', split_axis=1, concat_axis=3, tiled=True)  58.4 us
    unnamed x28, local copies, waits for them, and re-layouts  28.3 us
    psum x1, local copies, waits for them, and re-layouts, body(): summed = lax.psum(term, 'rcv')  14.3 us
    all_to_all x2, local copies, waits for them, and re-layouts, body(): lax.all_to_all(summed, 'freq', split_axis=3, concat_axis=1, tiled=True)  14 us
    all_to_all x1, other arithmetic, body(): lax.all_to_all(summed, 'freq', split_axis=3, concat_axis=1, tiled=True)  13.7 us
    dot_general x1, matrix products, forward_panel(): jnp.einsum('ual,uel->eua', reflection_imaginary, focusing_input[:, 1], pr...  11.1 us
  transfers between devices with their start and end apart: 3, of which 2 were waited for; matrix products, arithmetic and copies ran while one was open for 0% of the time, Pallas kernels for 0%

commit v1 on v0

--- a/solution.py
+++ b/solution.py
@@ -75,7 +75,7 @@
     cosine, sine_table = dft_tables(freqs, samples)
     share = mute_source.shape[0]
     term = forward_panel(reflection, focusing_input)
-    summed = lax.psum(term, "rcv")
+    summed = jnp.sum(lax.all_gather(term, "rcv"), axis=0)
     spectrum = lax.all_to_all(summed, "freq", split_axis=3, concat_axis=1, tiled=True)
     mutes_all = lax.all_gather(mute_source, "rcv", axis=0, tiled=True)
     windowed = window(to_time(spectrum, cosine, sine_table, factor), mutes_all)

time: 462 us -> 685 us (1.48)
  waiting for transfers between devices: 141 us -> 340 us
  other arithmetic: 16.8 us -> 39.8 us
    all_gather x0 -> x1, waiting for transfers between devices: none -> 331 us  [body(): summed = jnp.sum(lax.all_gather(term, 'rcv'), axis=0)]
    psum x1 -> x0, waiting for transfers between devices: 132 us -> none  [body(): summed = lax.psum(term, 'rcv')]
    reduce_sum x0 -> x1, other arithmetic: none -> 23 us  [body(): summed = jnp.sum(lax.all_gather(term, 'rcv'), axis=0)]
    psum x1 -> x0, local copies, waits for them, and re-layouts: 14.3 us -> none  [body(): summed = lax.psum(term, 'rcv')]
    reduce_sum x0 -> x1, local copies, waits for them, and re-layouts: none -> 14.3 us  [body(): summed = jnp.sum(lax.all_gather(term, 'rcv'), axis=0)]
where the time goes in v1:
time: 685 us; the launch traced here: 679 us
  waiting for transfers between devices  340 us (50%)
  blocking collectives  118 us (17%)
  matrix products  84 us (12%)
  local copies, waits for them, and re-layouts  71.9 us (10%)
  other arithmetic  39.8 us (6%)
  between operations  14.6 us (2%)
  starting transfers between devices  10.5 us (2%)
    all_gather x1, waiting for transfers between devices, body(): summed = jnp.sum(lax.all_gather(term, 'rcv'), axis=0)  331 us
    all_gather x1, blocking collectives, body(): mutes_all = lax.all_gather(mute_source, 'rcv', axis=0, tiled=True)  60 us
    all_to_all x1, blocking collectives, body(): lax.all_to_all(back_local, 'freq', split_axis=1, concat_axis=3, tiled=True)  58.4 us
    unnamed x28, local copies, waits for them, and re-layouts  28.3 us
    reduce_sum x1, other arithmetic, body(): summed = jnp.sum(lax.all_gather(term, 'rcv'), axis=0)  23 us
    reduce_sum x1, local copies, waits for them, and re-layouts, body(): summed = jnp.sum(lax.all_gather(term, 'rcv'), axis=0)  14.3 us
    all_to_all x2, local copies, waits for them, and re-layouts, body(): lax.all_to_all(summed, 'freq', split_axis=3, concat_axis=1, tiled=True)  14 us
  transfers between devices with their start and end apart: 3, of which 2 were waited for; matrix products, arithmetic and copies ran while one was open for 0% of the time, Pallas kernels for 0%

profile of v1, /device:TPU:0, one launch (start us, length us, event | category | flops | bytes accessed | tf_op | source)
XLA Modules:
  0.0 679.4 jit_solution(10258308595810735700)
XLA Ops:
  7.2 0.0 all-gather.4.cloned.1.call-start
  7.2 0.0 copy-start
  7.2 10.8 %fusion.4 = f32[16,32,1024]{2,1,0:T(8,128)S(1)} fusion(f32[16,2,1024,128]{3,2,1,0:T(8,128)} %param.5, f32[16,2,32,128]{3,2,1,0:T(8,128)} %param.6), kind=kOutput, calls=%fused_computation.4 | convolution fusion | flops 805306368 | bytes 10747904 | tf_op jit(solution)/shard_map/ual,uel->eua/dot_general | solution.py:36
  18.1 11.1 %fusion.6 = f32[16,32,1024]{2,1,0:T(8,128)S(1)} fusion(f32[16,2,1024,128]{3,2,1,0:T(8,128)} %param.5, f32[16,2,32,128]{3,2,1,0:T(8,128)S(1)} %copy-done.4), kind=kOutput, calls=%fused_computation.6 | convolution fusion | flops 805306368 | bytes 10747904 | tf_op jit(solution)/shard_map/ual,uel->eua/dot_general | solution.py:31
  29.2 0.0 copy-done
  29.2 8.4 %add_bitcast_fusion = f32[32,16,1,1024]{3,0,1,2:T(8,128)S(1)} fusion(f32[16,32,1024]{2,1,0:T(8,128)S(1)} %fusion.4, f32[16,2,1024,128]{3,2,1,0:T(8,128)S(1)} %copy-done, f32[16,2,32,128]{3,2,1,0:T(8,128)S(1)} %copy-done.4), kind=kOutput, calls=%fused_computation.38 | convolution fusion | flops 805830656 | bytes 12845056 | tf_op jit(solution)/shard_map/ual,uel->eua/dot_general | solution.py:34
  37.6 8.6 %subtract_bitcast_fusion = f32[32,16,1,1024]{3,0,1,2:T(8,128)S(1)} fusion(f32[16,32,1024]{2,1,0:T(8,128)S(1)} %fusion.6, f32[16,2,1024,128]{3,2,1,0:T(8,128)S(1)} %copy-done, f32[16,2,32,128]{3,2,1,0:T(8,128)S(1)} %copy-done.4), kind=kOutput, calls=%fused_computation.39 | convolution fusion | flops 805830656 | bytes 12845056 | tf_op jit(solution)/shard_map/ual,uel->eua/dot_general | solution.py:29
  46.2 2.6 pad_maximum_fusion
  48.8 0.0 all-gather.4.cloned.1.call-update
  48.8 331.2 %all-gather.4.cloned.1.call-done = f32[512,16,2,1024]{3,0,1,2:T(8,128)} async-done(((f32[32,16,2,1024]{3,0,1,2:T(8,128)}), f32[512,16,2,1024]{3,0,1,2:T(8,128)}) %all-gather.4.cloned.1.call-update) | async-done | bytes 67108880 | tf_op jit(solution)/shard_map/all_gather | solution.py:78
  380.1 23.0 %reduce_sum.9 = f32[32,16,2,1024]{3,0,1,2:T(8,128)} reduce(f32[16,32,16,2,1024]{4,1,0,2,3:T(8,128)} %bitcast.11, f32[]{:T(128)} %constant.16.clone.1), dimensions={0}, to_apply=%region_0.1 | reduce | flops 15728640 | bytes 71303168 | tf_op jit(solution)/shard_map/reduce_sum | solution.py:78
  403.1 14.3 %copy.50 = f32[32,16,2,1024]{0,1,2,3:T(8,128)} copy(f32[32,16,2,1024]{3,0,1,2:T(8,128)} %reduce_sum.9) | data formatting | bytes 8388608 | tf_op jit(solution)/shard_map/reduce_sum | solution.py:78
  417.4 12.8 %reshape.17 = f32[8,1,131072]{2,1,0:T(1,128)} reshape(f32[1024,2,16,32]{3,2,1,0:T(8,128)} %bitcast.142) | data formatting | bytes 8388608
  430.2 7.0 %all-to-all-start = ((f32[8,1,131072]{2,1,0:T(1,128)}), f32[8,1,131072]{2,1,0:T(1,128)}, u32[]{:S(2)}, u32[]{:S(2)}) async-start(f32[8,1,131072]{2,1,0:T(1,128)} %reshape.17), calls=%async_computation | async-start | bytes 8388608 | tf_op jit(solution)/shard_map/all_to_all | solution.py:79
  437.2 0.0 copy-done.7
  437.2 60.0 %all-gather.1 = s32[16,2,128]{2,1,0:T(2,128)S(1)} all-gather(s32[1,2,128]{2,1,0:T(2,128)S(1)} %bitcast.153), channel_id=1, replica_groups=mesh['freq'=8,'rcv'=16] {'rcv'}, dimensions={0}, use_global_device_ids=true | all-gather | bytes 17408 | tf_op jit(solution)/shard_map/all_gather | solution.py:80
  497.2 0.0 all-to-all-done
  497.2 0.5 broadcast.42
  497.7 13.7 %reduce = f32[8,131072]{1,0:T(8,128)} reduce(f32[8,1,131072]{2,1,0:T(1,128)} %all-to-all-done, f32[]{:T(128)} %broadcast.42), dimensions={1}, to_apply=%all_to_all.39.reduce_sub_computation | reduce | bytes 8388612 | tf_op jit(solution)/shard_map/all_to_all | solution.py:79
  511.4 13.4 %reshape.18 = f32[1024,2,16,32]{3,2,1,0:T(8,128)} reshape(f32[8,131072]{1,0:T(8,128)} %reduce) | data formatting | bytes 8388608
  524.8 13.5 %copy.52 = f32[32,8,16,2,128]{4,2,1,0,3:T(8,128)} copy(f32[32,8,16,2,128]{0,2,3,4,1:T(8,128)} %bitcast.143) | data formatting | bytes 8388608 | tf_op jit(solution)/shard_map/all_to_all | solution.py:79
  538.3 0.0 copy-start.3
  538.3 5.8 fusion.25
  544.1 5.0 multiply_select_fusion
  549.1 2.8 multiply_bitcast_fusion
  552.0 3.0 multiply_bitcast_fusion.1
  555.0 0.5 pad_maximum_fusion.1
  555.5 2.4 copy.55
  557.9 58.4 %all_to_all.54 = f32[32,128,2,128]{3,0,2,1:T(8,128)S(1)} all-to-all(f32[32,128,2,128]{3,0,2,1:T(8,128)S(1)} %copy.55), channel_id=1, replica_groups=mesh['freq'=8,'rcv'=16] {'freq'}, dimensions={1} | all-to-all | bytes 8388608 | tf_op jit(solution)/shard_map/all_to_all | solution.py:84
  616.3 5.8 copy.74
  622.1 4.9 all_to_all.46
  627.0 7.3 %fusion = f32[16,32,128]{2,1,0:T(8,128)S(1)} fusion(f32[16,2,1024,128]{3,2,1,0:T(8,128)} %param.5, f32[32,16,2,1024]{3,0,1,2:T(8,128)} %all_to_all.46), kind=kOutput, calls=%fused_computation | convolution fusion | flops 805306368 | bytes 10747904 | tf_op jit(solution)/shard_map/klh,lhc->klc/dot_general | solution.py:52
  634.3 0.0 slice-start.2
  634.3 7.3 %fusion.2 = f32[16,32,128]{2,1,0:T(8,128)S(1)} fusion(f32[16,2,1024,128]{3,2,1,0:T(8,128)} %param.5, f32[32,16,2,1024]{3,0,1,2:T(8,128)} %all_to_all.46), kind=kOutput, calls=%fused_computation.2 | convolution fusion | flops 805306368 | bytes 10747904 | tf_op jit(solution)/shard_map/klh,lhc->klc/dot_general | solution.py:47
  641.6 0.0 copy-done.2
  641.6 0.0 slice-start.3
  641.6 7.2 %fusion.42 = f32[32,16,1,128]{3,0,1,2:T(8,128)S(1)} fusion(f32[16,32,128]{2,1,0:T(8,128)S(1)} %fusion, f32[16,2,1024,128]{3,2,1,0:T(8,128)} %param.5, f32[32,16,2,1024]{3,0,1,2:T(8,128)S(1)} %copy-done.2), kind=kOutput, calls=%fused_computation.47 | convolution fusion | flops 805371904 | bytes 11010048 | tf_op jit(solution)/shard_map/klh,lhc->klc/dot_general | solution.py:50
  648.8 0.0 copy-start.6
  648.8 4.5 fusion.36
  653.3 0.0 copy-start.5
  653.4 1.1 copy.57
  654.5 3.5 all-to-all-start.2
  658.0 1.0 constant_dynamic-slice_fusion
  659.0 0.9 copy.60
  659.9 8.9 %all-to-all-done.2 = f32[32,16,2,128]{3,1,2,0:T(8,128)S(1)} async-done(((f32[32,16,2,128]{3,1,2,0:T(8,128)}), f32[32,16,2,128]{3,1,2,0:T(8,128)S(1)}, u32[]{:S(2)}, u32[]{:S(2)}) %all-to-all-start.2) | async-done | bytes 524320 | tf_op jit(solution)/shard_map/all_to_all | solution.py:86
  668.9 1.1 fusion.46
  669.9 1.2 fusion.32
  671.2 1.1 copy.61
  (21 shorter events, 0.1 us)
Async XLA Ops:
  7.2 10.9 %copy-start.4 = (f32[16,2,32,128]{3,2,1,0:T(8,128)S(1)}, f32[16,2,32,128]{3,2,1,0:T(8,128)}, u32[]{:S(2)}) copy-start(f32[16,2,32,128]{3,2,1,0:T(8,128)} %param.6) | copy-start | bytes 1572868
  7.2 372.9 %all-gather.4.cloned.1.call-start = ((), (), s32[]{:S(2)}) async-start(), calls=%async_computation.3 | async-start | bytes 71303168 | tf_op jit(solution)/shard_map/all_gather | solution.py:78
  7.2 22.0 %copy-start = (f32[16,2,1024,128]{3,2,1,0:T(8,128)S(1)}, f32[16,2,1024,128]{3,2,1,0:T(8,128)}, u32[]{:S(2)}) copy-start(f32[16,2,1024,128]{3,2,1,0:T(8,128)} %param.5) | copy-start | bytes 50331652
  430.2 7.0 %copy-start.7 = (s32[2,128]{1,0:T(2,128)S(1)}, s32[2,128]{1,0:T(2,128)}, u32[]{:S(2)}) copy-start(s32[2,128]{1,0:T(2,128)} %param.8) | copy-start | bytes 3076
  430.2 67.0 %all-to-all-start = ((f32[8,1,131072]{2,1,0:T(1,128)}), f32[8,1,131072]{2,1,0:T(1,128)}, u32[]{:S(2)}, u32[]{:S(2)}) async-start(f32[8,1,131072]{2,1,0:T(1,128)} %reshape.17), calls=%async_computation | async-start | bytes 8388608 | tf_op jit(solution)/shard_map/all_to_all | solution.py:79
  538.3 5.8 copy-start.3
  549.1 2.8 copy-start.1
  627.0 21.8 %slice-start = ((s8[16777216]{0:T(1024)(128)(4,1)}), s8[4194304]{0:T(1024)(128)(4,1)S(1)}, s32[]{:S(2)}) async-start(s8[16777216]{0:T(1024)(128)(4,1)} %bitcast.140), calls=%async_computation.4 | async-start | bytes 8388608
  627.0 21.8 %slice-start.1 = ((s8[16777216]{0:T(1024)(128)(4,1)}), s8[4194304]{0:T(1024)(128)(4,1)S(1)}, s32[]{:S(2)}) async-start(s8[16777216]{0:T(1024)(128)(4,1)} %bitcast.140), calls=%async_computation.5 | async-start | bytes 8388608
  634.3 7.3 %copy-start.2 = (f32[32,16,2,1024]{3,0,1,2:T(8,128)S(1)}, f32[32,16,2,1024]{3,0,1,2:T(8,128)}, u32[]{:S(2)}) copy-start(f32[32,16,2,1024]{3,0,1,2:T(8,128)} %all_to_all.46) | copy-start | bytes 12582916
  634.3 14.5 %slice-start.2 = ((s8[16777216]{0:T(1024)(128)(4,1)}), s8[4194304]{0:T(1024)(128)(4,1)S(1)}, s32[]{:S(2)}) async-start(s8[16777216]{0:T(1024)(128)(4,1)} %bitcast.140), calls=%async_computation.6 | async-start | bytes 8388608
  641.6 7.2 %slice-start.3 = ((s8[16777216]{0:T(1024)(128)(4,1)}), s8[4194304]{0:T(1024)(128)(4,1)S(1)}, s32[]{:S(2)}) async-start(s8[16777216]{0:T(1024)(128)(4,1)} %bitcast.140), calls=%async_computation.7 | async-start | bytes 8388608
  648.8 9.2 %copy-start.6 = (s32[4,128]{1,0:T(4,128)S(1)}, s32[4,128]{1,0:T(4,128)}, u32[]{:S(2)}) copy-start(s32[4,128]{1,0:T(4,128)} %param.9) | copy-start | bytes 6148
  653.3 16.6 %copy-start.5 = (f32[256,4,128]{2,1,0:T(4,128)S(1)}, f32[256,4,128]{2,1,0:T(4,128)}, u32[]{:S(2)}) copy-start(f32[256,4,128]{2,1,0:T(4,128)} %param.7) | copy-start | bytes 1572868
  654.5 14.4 %all-to-all-start.2 = ((f32[32,16,2,128]{3,1,2,0:T(8,128)}), f32[32,16,2,128]{3,1,2,0:T(8,128)S(1)}, u32[]{:S(2)}, u32[]{:S(2)}) async-start(f32[32,16,2,128]{3,1,2,0:T(8,128)} %copy.57), calls=%async_computation.2 | async-start | bytes 1048576 | tf_op jit(solution)/shard_map/all_to_all | solution.py:86
Sparse Core Ops, SparseCore 0:
  49.0 331.0 all-gather.3
